TPU v7x, 32 devices: a whole 2x2x4 slice. The times are simulated.
32 devices in a mesh: gx: 4 (over z), gy: 4 (over x, core), gz: 2 (over y).
Axes of the slice: x: 2, y: 2, z: 4, core: 2. Of those that a mesh axis runs over, the one named last changes fastest.
Arguments:
- features: float32 [4, 4, 2, 256, 256], P('gx', 'gy', 'gz'), may hold values from -6 to 6
- positions: float32 [4, 4, 2, 3, 256], P('gx', 'gy', 'gz'), may hold values from 0 to 1
- counts: int32 [4, 4, 2], P('gx', 'gy', 'gz'), may hold values from 51 to 256, as said below
- w_src: float32 [256, 256], replicated, may hold values from -0.375 to 0.375
- w_out: float32 [256, 256], replicated, may hold values from -0.375 to 0.375
- radial: float32 [8, 256], replicated, may hold values from -5 to 5
Outputs:
- updated: float32 [4, 4, 2, 256, 256], P('gx', 'gy', 'gz')
Inputs may be any that keep to these rules, and one draw needn't show every extreme that they name: The atoms of a bin fill its first counts slots; some bin is full in every draw, and some bins hold more than 128 atoms.
All inputs are finite; a program needn't handle non-finite values.
Results may differ from a plain program's by a relative error of at most 0.0003.
Values sent between devices are 32-bit elements; how exact they have to be, the bound alone decides.
A program may use at most 64 MiB of HBM per device.

v0:
```python
import math

import jax
import jax.numpy as jnp
import numpy as np
from jax import lax
from jax.experimental import pallas as pl
from jax.experimental.pallas import tpu as pltpu
from jax.sharding import PartitionSpec as P

BLK = 128
CHUNK = 256
far_value = 100.0
gamma_width = 10.0
message_scale = 0.125
highest = lax.Precision.HIGHEST
f32, bf16, i32 = jnp.float32, jnp.bfloat16, jnp.int32


def envelope_coefficients():
    t = np.cos(np.pi * (np.arange(64) + 0.5) / 64) * 0.5 + 0.5
    value = 0.5 * (np.cos(np.pi * np.sqrt(t)) + 1.0)
    fit = np.polynomial.chebyshev.Chebyshev.fit(t, value, 7, domain=[0, 1])
    return [float(c) for c in fit.convert(kind=np.polynomial.Polynomial).coef]


ENVELOPE = envelope_coefficients()


def split(value):
    high = value.astype(bf16)
    return high, (value - high.astype(f32)).astype(bf16)


def dot(a, b):
    return jnp.dot(a, b, preferred_element_type=f32)


def dot3(a, b):
    ah, al = split(a)
    bh, bl = split(b)
    return dot(ah, bh) + (dot(ah, bl) + dot(al, bh))


def project_kernel(count_ref, feats_ref, place_ref, w_ref, early_ref, later_ref):
    value = dot3(feats_ref[...], w_ref[...])
    cap = feats_ref.shape[0]
    count = count_ref[0]
    slot = lax.broadcasted_iota(i32, (1, cap), 1)
    early_ref[:BLK] = value[:BLK]
    early_ref[BLK : BLK + 3] = jnp.where(slot < count, place_ref[...], far_value)
    early_ref[BLK + 3 : BLK + 4] = jnp.broadcast_to(count.astype(f32), (1, cap))
    early_ref[BLK + 4 :] = jnp.zeros((4, cap), f32)
    later_ref[...] = value[BLK:]


def pairs_kernel(names, sizes, nrbf, *refs):
    kinds, slots = near_slots(sizes)
    tiles = len(slots) + 1
    mirrored = tuple(n == 2 for n in sizes)
    early_ref, later_ref, all_early, all_later, feats_ref, radial_ref, w_ref, out_ref = refs[:8]
    high_p, low_p, where_j, where_i, high_b, low_b, total, message = refs[8:]
    early = [early_ref] + [all_early.at[t] for t in range(tiles - 1)]
    later = [later_ref] + [all_later.at[t] for t in range(tiles - 1)]
    lane = lax.broadcasted_iota(i32, (8, BLK), 1)
    line = lax.broadcasted_iota(i32, (8, BLK), 0)
    places = [lax.axis_index(n) for n in names]

    def shift_of(t):
        shift = jnp.zeros((8, BLK), f32)
        for d in range(3):
            if t and slots[t - 1][d]:
                offset, mirror = slot_offset(kinds[d][slots[t - 1][d] - 1], places[d])
                shift = jnp.where(line == d, jnp.asarray(offset, i32).astype(f32), shift)
                shift = jnp.where(line == d + 4, float(mirror), shift)
        return shift

    counts = [jnp.max(t[BLK + 3 : BLK + 4, :BLK]).astype(i32) for t in early]
    own_blocks = (counts[0] + BLK - 1) // BLK

    def append(rows_ref, place, count, at):
        rows = (count + 15) // 16 * 16
        high, low = split(rows_ref[:BLK])
        at = pl.multiple_of(at, 16)
        high_p[pl.ds(at, BLK), :] = high
        low_p[pl.ds(at, BLK), :] = low
        turn = lax.rem(at, BLK)
        page = at // BLK
        rolled = pltpu.roll(place, turn, 1)
        where_j[page] = jnp.where(lane >= turn, rolled, where_j[page])
        where_j[page + 1] = rolled
        return at + rows

    at = jnp.int32(0)
    for half, source in ((0, early), (1, later)):
        for t in range(tiles):
            count = own_blocks * BLK if t == 0 else counts[t]
            here = jnp.clip(count - half * BLK, 0, BLK)
            place = early[t][BLK:, half * BLK : (half + 1) * BLK]
            shift = shift_of(t)
            if half:
                @pl.when(here > 0)
                def _():
                    append(source[t], place + shift, here, at)

                at = at + (here + 15) // 16 * 16
            else:
                at = append(source[t], place + shift, here, at)
            if t == 0 and half == 0:
                @pl.when(own_blocks > 1)
                def _():
                    append(later[0], early[0][BLK:, BLK:], jnp.int32(BLK), jnp.int32(BLK))

                at = own_blocks * BLK
                counts[0] = jnp.int32(0)
                own_count = own_blocks
                own_blocks = jnp.int32(0)
    own_blocks = own_count
    tail = pl.multiple_of(at, 16)
    zeros = jnp.zeros((CHUNK, high_p.shape[1]), bf16)
    high_p[pl.ds(tail, CHUNK), :] = zeros
    low_p[pl.ds(tail, CHUNK), :] = zeros
    far = jnp.where(line < 4, 2 * far_value, 0.0)
    page = at // BLK
    where_j[page] = jnp.where(lane >= lax.rem(at, BLK), far, where_j[page])
    where_j[page + 1] = far
    where_j[page + 2] = far
    chunks = (at + CHUNK - 1) // CHUNK
    difference = lax.broadcasted_iota(i32, (32, BLK), 0) - lax.broadcasted_iota(i32, (32, BLK), 1)

    message[...] = jnp.zeros_like(message)

    @pl.loop(0, own_blocks)
    def _(row_block):
        row = pl.multiple_of(row_block * BLK, BLK)
        mine = early_ref[BLK:, pl.ds(row, BLK)]
        for c in range(3):
            where_i[c] = jnp.broadcast_to(mine[c : c + 1], (BLK, BLK)).T
        total[...] = jnp.zeros_like(total)

        @pl.loop(0, chunks)
        def _(chunk):
            for half in range(CHUNK // BLK):
                theirs = where_j[chunk * (CHUNK // BLK) + half]
                gap = chunk * CHUNK + half * BLK - row
                for sub in range(0, BLK, 32):
                    square = None
                    for c in range(3):
                        delta = theirs[c : c + 1, :] - where_i[c, sub : sub + 32, :]
                        if mirrored[c]:
                            delta = theirs[c + 4 : c + 5, :] - jnp.abs(delta)
                        delta = delta * delta
                        square = delta if square is None else square + delta
                    reach = (square < 1.0) & (difference != gap - sub)
                    square = jnp.minimum(square, 1.0)
                    distance = square * lax.rsqrt(jnp.maximum(square, 1e-30))
                    envelope = jnp.full_like(square, ENVELOPE[-1])
                    for coefficient in ENVELOPE[-2::-1]:
                        envelope = envelope * square + coefficient
                    envelope = jnp.where(reach, envelope, 0.0)
                    step = gamma_width / nrbf
                    basis = envelope * jnp.exp(step * distance - gamma_width * square)
                    ratio = jnp.exp(2.0 * step * distance)
                    for k in range(nrbf):
                        if k:
                            basis = basis * ratio
                        high, low = split(basis)
                        spot = (slice(k * BLK + sub, k * BLK + sub + 32), slice(half * BLK, half * BLK + BLK))
                        high_b[spot] = high
                        low_b[spot] = low
            base = pl.multiple_of(chunk * CHUNK, CHUNK)
            ph = high_p[pl.ds(base, CHUNK), :]
            pw = low_p[pl.ds(base, CHUNK), :]
            bh = high_b[...]
            total[...] += dot(bh, ph) + (dot(bh, pw) + dot(low_b[...], ph))

        value = None
        for k in range(nrbf):
            weight = radial_ref[k : k + 1, :] * math.exp(-gamma_width * ((k + 0.5) / nrbf) ** 2)
            term = total[k * BLK : (k + 1) * BLK, :] * weight
            value = term if value is None else value + term
        message[pl.ds(row, BLK), :] = value * message_scale

    mixed = dot3(message[...], w_ref[...])
    out_ref[...] = feats_ref[...] + mixed / (1.0 + jnp.exp(-mixed))


def near_slots(sizes):
    kinds = []
    for axis, n in enumerate(sizes):
        if n == 2:
            kinds.append(("swap",))
        elif axis == 1 and n % 2 == 0:
            kinds.append(("cross", "partner"))
        else:
            kinds.append(("up", "down"))
    counts = [len(k) + 1 for k in kinds]
    slots = [(a, b, c) for a in range(counts[0]) for b in range(counts[1]) for c in range(counts[2])]
    return kinds, slots[1:]


def slot_offset(kind, index):
    side = 1 - 2 * lax.rem(index, 2)
    return {"swap": (0, 1), "cross": (-side, 0), "partner": (side, 0), "up": (-1, 0), "down": (1, 0)}[kind]


def routes(kinds):
    every = [[(axis, m) for m in range(len(kinds[axis]))] for axis in range(3)]
    first, last = every[1][:1], every[1][1:]
    return [
        [every[0], every[2], every[1]],
        [every[0], first, every[2], last],
        [every[0], every[2], every[1]],
        [first, every[2], every[0], last],
    ]


def halo_kernel(names, sizes, early_ref, later_ref, all_early, all_later, send_sem, recv_sem):
    kinds, slots = near_slots(sizes)
    width = early_ref.shape[1]
    half = width // 2
    places = [lax.axis_index(n) for n in names]

    def target(axis, m):
        n, at = sizes[axis], places[axis]
        side = 1 - 2 * lax.rem(at, 2)
        step = {"swap": 1, "cross": n - side, "partner": n + side, "up": 1, "down": n - 1}[kinds[axis][m]]
        return {names[axis]: lax.rem(at + step, n)}

    moves = [(axis, m) for axis in range(3) for m in range(len(kinds[axis]))]
    barrier = pltpu.get_barrier_semaphore()
    for move in moves:
        pl.semaphore_signal(barrier, inc=1, device_id=target(*move), device_id_type=pl.DeviceIdType.MESH)
    pl.semaphore_wait(barrier, len(moves))

    def piece(slot, number):
        own = (early_ref, later_ref)[number // 2]
        full = own if slot is None else (all_early, all_later)[number // 2].at[slot]
        return full.at[:, pl.ds(number % 2 * half, half)]

    held = [[(0, 0, 0)] for _ in range(4)]
    stages = routes(kinds)
    copies, arrived = {}, set()

    def arrive(slot, number):
        if slot != (0, 0, 0) and (slot, number) not in arrived:
            arrived.add((slot, number))
            copies[slot, number].wait_recv()

    for stage in range(max(len(r) for r in stages)):
        fresh = [[] for _ in range(4)]
        for number in range(4):
            if stage >= len(stages[number]):
                continue
            for source in held[number]:
                for axis, m in stages[number][stage]:
                    if source[axis] != 0:
                        continue
                    arrive(source, number)
                    goal = tuple(m + 1 if d == axis else source[d] for d in range(3))
                    to = slots.index(goal)
                    origin = None if source == (0, 0, 0) else slots.index(source)
                    copy = pltpu.make_async_remote_copy(
                        src_ref=piece(origin, number),
                        dst_ref=piece(to, number),
                        send_sem=send_sem.at[to, number],
                        recv_sem=recv_sem.at[to, number],
                        device_id=target(axis, m),
                        device_id_type=pl.DeviceIdType.MESH,
                    )
                    copy.start()
                    copies[goal, number] = copy
                    fresh[number].append(goal)
        for number in range(4):
            held[number] += fresh[number]
    for (slot, number), copy in copies.items():
        arrive(slot, number)
        copy.wait_send()


def local(features, positions, counts, w_src, w_out, radial):
    feats = features[0, 0, 0]
    cap, width = feats.shape
    nrbf = radial.shape[0]
    names = ("gx", "gy", "gz")
    early, later = pl.pallas_call(
        project_kernel,
        out_shape=(jax.ShapeDtypeStruct((BLK + 8, width), f32), jax.ShapeDtypeStruct((cap - BLK, width), f32)),
        in_specs=[pl.BlockSpec(memory_space=pltpu.SMEM)] + [pl.BlockSpec(memory_space=pltpu.VMEM)] * 3,
    )(counts.reshape(1), feats, positions[0, 0, 0], w_src)
    sizes = tuple(lax.axis_size(n) for n in names)
    kinds, slots = near_slots(sizes)
    near = len(slots)
    total = near + 1
    all_early, all_later = pl.pallas_call(
        lambda *refs: halo_kernel(names, sizes, *refs),
        out_shape=(jax.ShapeDtypeStruct((near, *early.shape), f32), jax.ShapeDtypeStruct((near, *later.shape), f32)),
        in_specs=[pl.BlockSpec(memory_space=pl.ANY)] * 2,
        out_specs=(pl.BlockSpec(memory_space=pl.ANY),) * 2,
        scratch_shapes=[pltpu.SemaphoreType.DMA((near, 4)), pltpu.SemaphoreType.DMA((near, 4))],
        compiler_params=pltpu.CompilerParams(collective_id=0, has_side_effects=True),
    )(early, later)
    room = total * cap + 2 * CHUNK
    out = pl.pallas_call(
        lambda *refs: pairs_kernel(names, sizes, nrbf, *refs),
        out_shape=jax.ShapeDtypeStruct((cap, width), f32),
        scratch_shapes=[
            pltpu.VMEM((room, width), bf16),
            pltpu.VMEM((room, width), bf16),
            pltpu.VMEM((room // BLK + 2, 8, BLK), f32),
            pltpu.VMEM((3, BLK, BLK), f32),
            pltpu.VMEM((nrbf * BLK, CHUNK), bf16),
            pltpu.VMEM((nrbf * BLK, CHUNK), bf16),
            pltpu.VMEM((nrbf * BLK, width), f32),
            pltpu.VMEM((cap, width), f32),
        ],
        compiler_params=pltpu.CompilerParams(vmem_limit_bytes=56 << 20),
    )(early, later, all_early, all_later, feats, radial, w_out)
    return out[None, None, None]


def solution(mesh):
    in_specs = (P("gx", "gy", "gz", None, None), P("gx", "gy", "gz", None, None), P("gx", "gy", "gz"), P(), P(), P())
    return jax.shard_map(local, mesh=mesh, in_specs=in_specs, out_specs=P("gx", "gy", "gz", None, None), check_vma=False)
```

profile of v0, /device:TPU:19, one launch (start us, length us, event | category | flops | bytes accessed | tf_op | source)
XLA Modules:
  0.0 57.3 jit_solution(7390584062923594432)
XLA Ops:
  0.7 1.3 %copy.9 = f32[1,1,1,3,256]{4,3,2,1,0:T(4,128)} copy(f32[1,1,1,3,256]{4,2,3,1,0:T(1,128)} %param.7) | data formatting | bytes 6144
  1.9 2.0 %shard_map.64 = (f32[136,256]{1,0:T(8,128)}, f32[128,256]{1,0:T(8,128)}) custom-call(s32[1]{0:T(128)} %bitcast.6.count_ref, f32[256,256]{1,0:T(8,128)} %bitcast.7, f32[3,256]{1,0:T(4,128)} %bitcast.9, f32[256,256]{1,0:T(8,128)} %w_ref.1), custom_call_target="tpu_custom_call" | custom-call | tf_op jit(solution)/shard_map/pallas_call | solution.py:286
  3.9 33.0 %shard_map.65 = (f32[17,136,256]{2,1,0:T(8,128)}, f32[17,128,256]{2,1,0:T(8,128)}) custom-call(f32[136,256]{1,0:T(8,128)} %get-tuple-element.9.refs_0_, f32[128,256]{1,0:T(8,128)} %get-tuple-element.10.refs_1_), custom_call_target="tpu_custom_call" | custom-call | tf_op jit(solution)/shard_map/pallas_call | solution.py:295
  36.9 20.3 %shard_map.66 = f32[256,256]{1,0:T(8,128)} custom-call(f32[136,256]{1,0:T(8,128)} %get-tuple-element.9.refs_0_, f32[128,256]{1,0:T(8,128)} %get-tuple-element.10.refs_1_, f32[17,136,256]{2,1,0:T(8,128)} %get-tuple-element.11.refs_2_, f32[17,128,256]{2,1,0:T(8,128)} %get-tuple-element.12.refs_3_, f32[256,256]{1,0:T(8,128)} %bitcast.8, f32[8,256]{1,0:T(8,128)} %refs_5_.1, ...), custom_call_target="tpu_custom_call" | custom-call | tf_op jit(solution)/shard_map/pallas_call | solution.py:304
where the time goes:
time: 56.2 us; the launch traced here: 57.3 us
  Pallas kernels  55.3 us (98%)
  local copies, waits for them, and re-layouts  1.28 us (2%)
  between operations  0.66 us (1%)
    pallas_call x1, Pallas kernels, local(): pl.pallas_call(lambda *refs: halo_kernel(names, sizes, *refs), out_shape=...  33 us
    pallas_call x1, Pallas kernels, local(): pl.pallas_call(lambda *refs: pairs_kernel(names, sizes, nrbf, *refs), out...  20.3 us
    pallas_call x1, Pallas kernels, local(): pl.pallas_call(project_kernel, out_shape=(jax.ShapeDtypeStruct((BLK + 8,...  2 us
    unnamed x1, local copies, waits for them, and re-layouts  1.28 us

commit v1 on v0

--- a/solution.py
+++ b/solution.py
@@ -10,6 +10,7 @@
 
 BLK = 128
 CHUNK = 256
+PART = 32
 far_value = 100.0
 gamma_width = 10.0
 message_scale = 0.125
@@ -46,9 +47,8 @@
     value = dot3(feats_ref[...], w_ref[...])
     cap = feats_ref.shape[0]
     count = count_ref[0]
-    slot = lax.broadcasted_iota(i32, (1, cap), 1)
     early_ref[:BLK] = value[:BLK]
-    early_ref[BLK : BLK + 3] = jnp.where(slot < count, place_ref[...], far_value)
+    early_ref[BLK : BLK + 3] = place_ref[...]
     early_ref[BLK + 3 : BLK + 4] = jnp.broadcast_to(count.astype(f32), (1, cap))
     early_ref[BLK + 4 :] = jnp.zeros((4, cap), f32)
     later_ref[...] = value[BLK:]
@@ -59,7 +59,7 @@
     tiles = len(slots) + 1
     mirrored = tuple(n == 2 for n in sizes)
     early_ref, later_ref, all_early, all_later, feats_ref, radial_ref, w_ref, out_ref = refs[:8]
-    high_p, low_p, where_j, where_i, high_b, low_b, total, message = refs[8:]
+    high_p, low_p, where_j, where_i, total, message, *parts = refs[8:]
     early = [early_ref] + [all_early.at[t] for t in range(tiles - 1)]
     later = [later_ref] + [all_later.at[t] for t in range(tiles - 1)]
     lane = lax.broadcasted_iota(i32, (8, BLK), 1)
@@ -140,46 +140,52 @@
 
         @pl.loop(0, chunks)
         def _(chunk):
-            for half in range(CHUNK // BLK):
-                theirs = where_j[chunk * (CHUNK // BLK) + half]
-                gap = chunk * CHUNK + half * BLK - row
-                for sub in range(0, BLK, 32):
-                    square = None
-                    for c in range(3):
-                        delta = theirs[c : c + 1, :] - where_i[c, sub : sub + 32, :]
-                        if mirrored[c]:
-                            delta = theirs[c + 4 : c + 5, :] - jnp.abs(delta)
-                        delta = delta * delta
-                        square = delta if square is None else square + delta
-                    reach = (square < 1.0) & (difference != gap - sub)
-                    square = jnp.minimum(square, 1.0)
-                    distance = square * lax.rsqrt(jnp.maximum(square, 1e-30))
-                    envelope = jnp.full_like(square, ENVELOPE[-1])
-                    for coefficient in ENVELOPE[-2::-1]:
-                        envelope = envelope * square + coefficient
-                    envelope = jnp.where(reach, envelope, 0.0)
-                    step = gamma_width / nrbf
-                    basis = envelope * jnp.exp(step * distance - gamma_width * square)
-                    ratio = jnp.exp(2.0 * step * distance)
-                    for k in range(nrbf):
-                        if k:
-                            basis = basis * ratio
-                        high, low = split(basis)
-                        spot = (slice(k * BLK + sub, k * BLK + sub + 32), slice(half * BLK, half * BLK + BLK))
-                        high_b[spot] = high
-                        low_b[spot] = low
             base = pl.multiple_of(chunk * CHUNK, CHUNK)
-            ph = high_p[pl.ds(base, CHUNK), :]
-            pw = low_p[pl.ds(base, CHUNK), :]
-            bh = high_b[...]
-            total[...] += dot(bh, ph) + (dot(bh, pw) + dot(low_b[...], ph))
-
-        value = None
-        for k in range(nrbf):
-            weight = radial_ref[k : k + 1, :] * math.exp(-gamma_width * ((k + 0.5) / nrbf) ** 2)
-            term = total[k * BLK : (k + 1) * BLK, :] * weight
-            value = term if value is None else value + term
-        message[pl.ds(row, BLK), :] = value * message_scale
+            pages = [where_j[chunk * (CHUNK // BLK) + half] for half in range(CHUNK // BLK)]
+            for part in range(BLK // PART):
+                high_b, low_b = parts[2 * part : 2 * part + 2]
+                for half in range(CHUNK // BLK):
+                    theirs = pages[half]
+                    gap = chunk * CHUNK + half * BLK - row
+                    for sub in range(0, PART, 32):
+                        first = part * PART + sub
+                        square = None
+                        for c in range(3):
+                            delta = theirs[c : c + 1, :] - where_i[c, first : first + 32, :]
+                            if mirrored[c]:
+                                delta = theirs[c + 4 : c + 5, :] - jnp.abs(delta)
+                            delta = delta * delta
+                            square = delta if square is None else square + delta
+                        reach = (square < 1.0) & (difference != gap - first)
+                        square = jnp.minimum(square, 1.0)
+                        distance = square * lax.rsqrt(jnp.maximum(square, 1e-30))
+                        envelope = jnp.full_like(square, ENVELOPE[-1])
+                        for coefficient in ENVELOPE[-2::-1]:
+                            envelope = envelope * square + coefficient
+                        envelope = jnp.where(reach, envelope, 0.0)
+                        step = gamma_width / nrbf
+                        basis = envelope * jnp.exp(step * distance - gamma_width * square)
+                        ratio = jnp.exp(2.0 * step * distance)
+                        for k in range(nrbf):
+                            if k:
+                                basis = basis * ratio
+                            high, low = split(basis)
+                            spot = (slice(k * PART + sub, k * PART + sub + 32), slice(half * BLK, half * BLK + BLK))
+                            high_b[spot] = high
+                            low_b[spot] = low
+                ph = high_p[pl.ds(base, CHUNK), :]
+                pw = low_p[pl.ds(base, CHUNK), :]
+                bh = high_b[...]
+                left = jnp.concatenate([bh, bh, low_b[...]], axis=1)
+                total[part] += dot(left, jnp.concatenate([ph, pw, ph], axis=0))
+
+        for part in range(BLK // PART):
+            value = None
+            for k in range(nrbf):
+                weight = radial_ref[k : k + 1, :] * math.exp(-gamma_width * ((k + 0.5) / nrbf) ** 2)
+                term = total[part, k * PART : (k + 1) * PART, :] * weight
+                value = term if value is None else value + term
+            message[pl.ds(row + part * PART, PART), :] = value * message_scale
 
     mixed = dot3(message[...], w_ref[...])
     out_ref[...] = feats_ref[...] + mixed / (1.0 + jnp.exp(-mixed))
@@ -238,8 +244,18 @@
         full = own if slot is None else (all_early, all_later)[number // 2].at[slot]
         return full.at[:, pl.ds(number % 2 * half, half)]
 
-    held = [[(0, 0, 0)] for _ in range(4)]
-    stages = routes(kinds)
+    plan = []
+    for number, route in enumerate(routes(kinds)):
+        held = [((0, 0, 0), 0)]
+        for stage, moved in enumerate(route):
+            fresh = []
+            for source, depth in held:
+                for axis, m in moved:
+                    if source[axis] == 0:
+                        goal = tuple(m + 1 if d == axis else source[d] for d in range(3))
+                        plan.append((depth, stage, number, source, goal, axis, m))
+                        fresh.append((goal, depth + 1))
+            held += fresh
     copies, arrived = {}, set()
 
     def arrive(slot, number):
@@ -247,32 +263,20 @@
             arrived.add((slot, number))
             copies[slot, number].wait_recv()
 
-    for stage in range(max(len(r) for r in stages)):
-        fresh = [[] for _ in range(4)]
-        for number in range(4):
-            if stage >= len(stages[number]):
-                continue
-            for source in held[number]:
-                for axis, m in stages[number][stage]:
-                    if source[axis] != 0:
-                        continue
-                    arrive(source, number)
-                    goal = tuple(m + 1 if d == axis else source[d] for d in range(3))
-                    to = slots.index(goal)
-                    origin = None if source == (0, 0, 0) else slots.index(source)
-                    copy = pltpu.make_async_remote_copy(
-                        src_ref=piece(origin, number),
-                        dst_ref=piece(to, number),
-                        send_sem=send_sem.at[to, number],
-                        recv_sem=recv_sem.at[to, number],
-                        device_id=target(axis, m),
-                        device_id_type=pl.DeviceIdType.MESH,
-                    )
-                    copy.start()
-                    copies[goal, number] = copy
-                    fresh[number].append(goal)
-        for number in range(4):
-            held[number] += fresh[number]
+    for _, _, number, source, goal, axis, m in sorted(plan, key=lambda p: p[:3]):
+        arrive(source, number)
+        to = slots.index(goal)
+        origin = None if source == (0, 0, 0) else slots.index(source)
+        copy = pltpu.make_async_remote_copy(
+            src_ref=piece(origin, number),
+            dst_ref=piece(to, number),
+            send_sem=send_sem.at[to, number],
+            recv_sem=recv_sem.at[to, number],
+            device_id=target(axis, m),
+            device_id_type=pl.DeviceIdType.MESH,
+        )
+        copy.start()
+        copies[goal, number] = copy
     for (slot, number), copy in copies.items():
         arrive(slot, number)
         copy.wait_send()
@@ -282,12 +286,14 @@
     feats = features[0, 0, 0]
     cap, width = feats.shape
     nrbf = radial.shape[0]
+    slot = lax.broadcasted_iota(i32, (1, cap), 1)
+    placed = jnp.where(slot < counts[0, 0, 0], positions[0, 0, 0], far_value)
     names = ("gx", "gy", "gz")
     early, later = pl.pallas_call(
         project_kernel,
         out_shape=(jax.ShapeDtypeStruct((BLK + 8, width), f32), jax.ShapeDtypeStruct((cap - BLK, width), f32)),
         in_specs=[pl.BlockSpec(memory_space=pltpu.SMEM)] + [pl.BlockSpec(memory_space=pltpu.VMEM)] * 3,
-    )(counts.reshape(1), feats, positions[0, 0, 0], w_src)
+    )(counts.reshape(1), feats, placed, w_src)
     sizes = tuple(lax.axis_size(n) for n in names)
     kinds, slots = near_slots(sizes)
     near = len(slots)
@@ -309,10 +315,9 @@
             pltpu.VMEM((room, width), bf16),
             pltpu.VMEM((room // BLK + 2, 8, BLK), f32),
             pltpu.VMEM((3, BLK, BLK), f32),
-            pltpu.VMEM((nrbf * BLK, CHUNK), bf16),
-            pltpu.VMEM((nrbf * BLK, CHUNK), bf16),
-            pltpu.VMEM((nrbf * BLK, width), f32),
+            pltpu.VMEM((BLK // PART, nrbf * PART, width), f32),
             pltpu.VMEM((cap, width), f32),
+            *[pltpu.VMEM((nrbf * PART, CHUNK), bf16) for _ in range(2 * (BLK // PART))],
         ],
         compiler_params=pltpu.CompilerParams(vmem_limit_bytes=56 << 20),
     )(early, later, all_early, all_later, feats, radial, w_out)

time: 56.2 us -> 53.6 us (0.954)
  the two profiles are of different devices: /device:TPU:19 before, /device:TPU:7 now
where the time goes in v1:
time: 53.6 us; the launch traced here: 53.3 us
  Pallas kernels  51.3 us (96%)
  other arithmetic  1.29 us (2%)
  between operations  0.67 us (1%)
    pallas_call x1, Pallas kernels, local(): pl.pallas_call(lambda *refs: halo_kernel(names, sizes, *refs), out_shape=...  31.4 us
    pallas_call x1, Pallas kernels, local(): pl.pallas_call(lambda *refs: pairs_kernel(names, sizes, nrbf, *refs), out...  17.9 us
    pallas_call x1, Pallas kernels, local(): pl.pallas_call(project_kernel, out_shape=(jax.ShapeDtypeStruct((BLK + 8,...  2 us
    select_n x1, other arithmetic, local(): placed = jnp.where(slot < counts[0, 0, 0], positions[0, 0, 0], far_value)  1.28 us

profile of v1, /device:TPU:7, one launch (start us, length us, event | category | flops | bytes accessed | tf_op | source)
XLA Modules:
  0.0 53.3 jit_solution(6806960071710200448)
XLA Ops:
  0.7 1.3 %bitcast_select_fusion.place_ref = f32[3,256]{1,0:T(4,128)} fusion(f32[1,1,1,3,256]{4,2,3,1,0:T(1,128)} %param.7, pred[256]{0:T(512)(128)(4,1)S(1)} %iota_compare_fusion), kind=kLoop, calls=%fused_computation | loop fusion | flops 768 | bytes 6400 | tf_op jit(solution)/shard_map/jit(_where)/select_n | solution.py:290
  1.9 2.0 %shard_map.64 = (f32[136,256]{1,0:T(8,128)}, f32[128,256]{1,0:T(8,128)}) custom-call(s32[1]{0:T(128)} %bitcast.6.count_ref, f32[256,256]{1,0:T(8,128)} %bitcast.8, f32[3,256]{1,0:T(4,128)} %bitcast_select_fusion.place_ref, f32[256,256]{1,0:T(8,128)} %w_ref.1), custom_call_target="tpu_custom_call" | custom-call | tf_op jit(solution)/shard_map/pallas_call | solution.py:292
  3.9 31.4 %shard_map.65 = (f32[17,136,256]{2,1,0:T(8,128)}, f32[17,128,256]{2,1,0:T(8,128)}) custom-call(f32[136,256]{1,0:T(8,128)} %get-tuple-element.9.refs_0_, f32[128,256]{1,0:T(8,128)} %get-tuple-element.10.refs_1_), custom_call_target="tpu_custom_call" | custom-call | tf_op jit(solution)/shard_map/pallas_call | solution.py:301
  35.4 17.9 %shard_map.66 = f32[256,256]{1,0:T(8,128)} custom-call(f32[136,256]{1,0:T(8,128)} %get-tuple-element.9.refs_0_, f32[128,256]{1,0:T(8,128)} %get-tuple-element.10.refs_1_, f32[17,136,256]{2,1,0:T(8,128)} %get-tuple-element.11.refs_2_, f32[17,128,256]{2,1,0:T(8,128)} %get-tuple-element.12.refs_3_, f32[256,256]{1,0:T(8,128)} %bitcast.9, f32[8,256]{1,0:T(8,128)} %refs_5_.1, ...), custom_call_target="tpu_custom_call" | custom-call | tf_op jit(solution)/shard_map/pallas_call | solution.py:310
  (1 shorter events, 0.0 us)
